TPU v7x, 256 devices: a whole 4x4x8 slice. The times are simulated.
256 devices in a mesh: atom: 32 (over y, z_hi, core), sample: 8 (over z_lo, x).
Axes of the slice: x: 4, y: 4, z: 8 (z_hi: 4, z_lo: 2; z = z_hi * 2 + z_lo), core: 2. Of those that a mesh axis runs over, the one named last changes fastest.
Arguments:
- atom_act: bfloat16 [16, 8192, 128], P('sample', 'atom'), may hold values from -3 to 3
- atom_cond: bfloat16 [8192, 128], P('atom'), may hold values from -6 to 6
- ref_pos: float32 [3, 8192], P(None, 'atom'), may hold values from -9 to 9
- atom_token: int32 [8192], P('atom'), may hold values from 0 to 340, never falling along the last dimension, each value on 1 to 48 neighbouring positions
- w_pair_in: float32 [16, 5], replicated, may hold values from -2.5 to 2.5
- w_rel: float32 [16, 9], replicated, may hold values from -6 to 6
- w_cond_pair: bfloat16 [2, 128, 16], replicated, may hold values from -1 to 1
- w_pair_mlp: float32 [3, 16, 16], replicated, may hold values from -1.5 to 1.5
- w_bias: float32 [3, 4, 16], replicated, may hold values from -6 to 6
- w_cond: bfloat16 [3, 128, 768], replicated, may hold values from -0.5 to 0.5
- w_attn: bfloat16 [3, 128, 512], replicated, may hold values from -0.5 to 0.5
- q_bias: float32 [3, 128], replicated, may hold values from -48 to 48
- w_out: bfloat16 [3, 128, 128], replicated, may hold values from -1 to 1
- w_up: bfloat16 [3, 128, 512], replicated, may hold values from -0.5 to 0.5
- w_down: bfloat16 [3, 256, 128], replicated, may hold values from -0.375 to 0.375
Outputs:
- atom_out: bfloat16 [16, 8192, 128], P('sample', 'atom')
Inputs may be any that keep to these rules, and one draw needn't show every extreme that they name: `atom_token`: atoms of one token are consecutive and token numbers never fall along the atoms; a token has 1 to 48 atoms.
All inputs are finite; a program needn't handle non-finite values.
Results may differ from a plain program's by a relative error of at most 0.023.
The roundings to bfloat16 on the way count: a program that leaves them out, or rounds other values in their place, can miss the bound.
Values may be sent and summed in bfloat16 or wider, within the bound.
A program may use at most 64 MiB of HBM per device.

v0:
```python
import jax
import jax.numpy as jnp
from jax import lax
from jax.sharding import PartitionSpec as P

QW = 32
KW = 128
REL_CLIP = 4
NREL = 9


def with_halo(block, sides, width):
    for axis, dim in sides:
        count = lax.axis_size(axis)
        forward = [(i, i + 1) for i in range(count - 1)]
        backward = [(target, source) for source, target in forward]
        low = lax.ppermute(
            lax.slice_in_dim(block, block.shape[dim] - width, None, axis=dim), axis, forward
        )
        high = lax.ppermute(lax.slice_in_dim(block, 0, width, axis=dim), axis, backward)
        block = jnp.concatenate([low, block, high], axis=dim)
    return block


def layer_norm(values):
    average = jnp.mean(values, axis=-1, keepdims=True)
    centered = values - average
    variance = jnp.mean(centered * centered, axis=-1, keepdims=True)
    return centered * lax.rsqrt(variance + 1e-05)


def key_windows(padded, window_count, along):
    shifts = KW // QW
    new_shape = padded.shape[:along] + (window_count + shifts - 1, QW) + padded.shape[along + 1 :]
    blocks = padded.reshape(new_shape)
    pieces = [
        lax.slice_in_dim(blocks, start_at, start_at + window_count, axis=along)
        for start_at in range(shifts)
    ]
    stacked = jnp.stack(pieces, axis=along + 1)
    return stacked.reshape(padded.shape[:along] + (window_count, KW) + padded.shape[along + 1 :])


def pair_bias(query_feats, key_feats, key_valid, w_pair_in, w_rel, w_pair_mlp, w_bias):
    highest = lax.Precision.HIGHEST
    differences = query_feats[0:3][:, :, :, None] - key_feats[0:3][:, :, None, :]
    query_tok = query_feats[3][:, :, None]
    key_tok = key_feats[3][:, None, :]
    same_token = jnp.where((query_tok == key_tok) & key_valid[:, None, :], 1.0, 0.0).astype(
        jnp.float32
    )
    inverse = 1.0 / (1.0 + jnp.sum(differences * differences, axis=0))
    token_gap = jnp.clip(key_tok - query_tok, -REL_CLIP, REL_CLIP)
    classes = jnp.arange(NREL, dtype=jnp.float32) - REL_CLIP
    one_hot = jnp.where(token_gap[None] == classes[:, None, None, None], 1.0, 0.0).astype(
        jnp.float32
    )
    pair_rep = (
        jnp.einsum("cx,xwqk->cwqk", w_pair_in[:, 0:3], differences, precision=highest)
        * same_token[None]
    )
    pair_rep = pair_rep + w_pair_in[:, 3][:, None, None, None] * (inverse * same_token)[None]
    pair_rep = pair_rep + w_pair_in[:, 4][:, None, None, None] * same_token[None]
    pair_rep = pair_rep + jnp.einsum("cr,rwqk->cwqk", w_rel, one_hot, precision=highest)
    pair_rep = pair_rep + query_feats[4:][:, :, :, None] + key_feats[4:][:, :, None, :]
    hidden = jax.nn.relu(
        jnp.einsum("dc,cwqk->dwqk", w_pair_mlp[0], jax.nn.relu(pair_rep), precision=highest)
    )
    hidden = jax.nn.relu(jnp.einsum("dc,cwqk->dwqk", w_pair_mlp[1], hidden, precision=highest))
    pair_rep = pair_rep + jnp.einsum("dc,cwqk->dwqk", w_pair_mlp[2], hidden, precision=highest)
    average = jnp.mean(pair_rep, axis=0, keepdims=True)
    centered = pair_rep - average
    variance = jnp.mean(centered * centered, axis=0, keepdims=True)
    normed = centered * lax.rsqrt(jnp.maximum(variance, 0.1))
    return jnp.einsum("lhc,cwqk->lwhqk", w_bias, normed, precision=highest).astype(jnp.bfloat16)


def local(
    atom_act,
    atom_cond,
    ref_pos,
    atom_token,
    w_pair_in,
    w_rel,
    w_cond_pair,
    w_pair_mlp,
    w_bias,
    w_cond,
    w_attn,
    q_bias,
    w_out,
    w_up,
    w_down,
):
    samples, local_atoms, channels = atom_act.shape
    window_count = local_atoms // QW
    head_count = w_bias.shape[1]
    head_dim = channels // head_count
    halo_width = (KW - QW) // 2
    shifts = KW // QW
    hidden_units = w_down.shape[1]
    atom_rank = lax.axis_index("atom")
    total_atoms = local_atoms * lax.axis_size("atom")
    tokens = atom_token.astype(jnp.float32)
    active = jax.nn.relu(atom_cond)
    query_cond = jnp.einsum("ac,cp->pa", active, w_cond_pair[0], preferred_element_type=jnp.float32)
    key_cond = jnp.einsum("ac,cp->pa", active, w_cond_pair[1], preferred_element_type=jnp.float32)
    query_table = jnp.concatenate([ref_pos, tokens[None], query_cond], axis=0)
    key_table = jnp.concatenate([ref_pos, tokens[None], key_cond], axis=0)
    feature_rows = query_table.shape[0]
    key_padded = with_halo(key_table, (("atom", 1),), halo_width)
    position = (
        atom_rank * local_atoms
        - halo_width
        + jnp.arange(window_count)[:, None] * QW
        + jnp.arange(KW)[None, :]
    )
    key_valid = (position >= 0) & (position < total_atoms)
    query_windows = query_table.reshape(feature_rows, window_count, QW)
    share_count = window_count // lax.axis_size("sample")
    first_window = lax.axis_index("sample") * share_count
    my_queries = lax.dynamic_slice_in_dim(query_windows, first_window, share_count, 1)
    key_block = lax.dynamic_slice_in_dim(
        key_padded, first_window * QW, (share_count + shifts - 1) * QW, 1
    )
    my_keys = key_windows(key_block, share_count, 1)
    my_valid = lax.dynamic_slice_in_dim(key_valid, first_window, share_count, 0)
    my_bias = pair_bias(my_queries, my_keys, my_valid, w_pair_in, w_rel, w_pair_mlp, w_bias)
    attn_bias = lax.all_gather(my_bias, "sample", axis=1, tiled=True)
    scale_factor = head_dim ** (-0.5)
    residual = atom_act.astype(jnp.float32)
    for layer_index in range(w_attn.shape[0]):
        cond_values = jnp.dot(atom_cond, w_cond[layer_index], preferred_element_type=jnp.float32)
        modulated = (
            jax.nn.sigmoid(cond_values[:, 0:channels]) * layer_norm(residual)
            + cond_values[:, channels : 2 * channels]
        ).astype(jnp.bfloat16)
        weights = w_attn[layer_index]
        projected = jnp.einsum(
            "sac,cf->saf", modulated, weights, preferred_element_type=jnp.float32
        )
        queries = (projected[..., 0:channels] + q_bias[layer_index]).astype(jnp.bfloat16)
        gating = jax.nn.sigmoid(projected[..., 3 * channels : 4 * channels])
        keyval = projected[..., channels : 3 * channels].astype(jnp.bfloat16)
        keyval_padded = with_halo(keyval, (("atom", 1),), halo_width)
        keyval_windows = key_windows(keyval_padded, window_count, 1)
        query_heads = queries.reshape(samples, window_count, QW, head_count, head_dim)
        key_heads = keyval_windows[..., 0:channels].reshape(
            samples, window_count, KW, head_count, head_dim
        )
        value_heads = keyval_windows[..., channels : 2 * channels].reshape(
            samples, window_count, KW, head_count, head_dim
        )
        scores = (
            jnp.einsum(
                "swqhd,swkhd->swhqk", query_heads, key_heads, preferred_element_type=jnp.float32
            )
            * scale_factor
        )
        scores = scores + attn_bias[layer_index][None].astype(jnp.float32)
        scores = jnp.where(key_valid[None, :, None, None, :], scores, -jnp.inf)
        row_max = jnp.max(scores, axis=-1, keepdims=True)
        exponent = jnp.exp(scores - row_max)
        attn_probs = (exponent / jnp.sum(exponent, axis=-1, keepdims=True)).astype(jnp.bfloat16)
        mixed_out = jnp.einsum(
            "swhqk,swkhd->swqhd", attn_probs, value_heads, preferred_element_type=jnp.float32
        ).reshape(samples, local_atoms, channels)
        mixed_out = (mixed_out * gating).astype(jnp.bfloat16)
        attended = jnp.einsum(
            "sac,cd->sad", mixed_out, w_out[layer_index], preferred_element_type=jnp.float32
        )
        residual = residual + jax.nn.sigmoid(cond_values[:, 2 * channels : 3 * channels]) * attended
        modulated2 = (
            jax.nn.sigmoid(cond_values[:, 3 * channels : 4 * channels]) * layer_norm(residual)
            + cond_values[:, 4 * channels : 5 * channels]
        ).astype(jnp.bfloat16)
        up_values = jnp.einsum(
            "sac,cf->saf", modulated2, w_up[layer_index], preferred_element_type=jnp.float32
        )
        hidden = (
            jax.nn.silu(up_values[..., 0:hidden_units])
            * up_values[..., hidden_units : 2 * hidden_units]
        ).astype(jnp.bfloat16)
        transition = jnp.einsum(
            "saf,fc->sac", hidden, w_down[layer_index], preferred_element_type=jnp.float32
        )
        residual = (
            residual + jax.nn.sigmoid(cond_values[:, 5 * channels : 6 * channels]) * transition
        )
    return residual.astype(jnp.bfloat16)


def solution(mesh):
    in_specs = (
        P("sample", "atom", None),
        P("atom", None),
        P(None, "atom"),
        P("atom"),
        P(),
        P(),
        P(),
        P(),
        P(),
        P(),
        P(),
        P(),
        P(),
        P(),
        P(),
    )
    out_specs = P("sample", "atom", None)
    return jax.shard_map(local, mesh=mesh, in_specs=in_specs, out_specs=out_specs, check_vma=False)
```

profile of v0, /device:TPU:30, one launch (start us, length us, event | category | flops | bytes accessed | tf_op | source)
XLA Modules:
  0.0 158.6 jit_solution(17236440815866380441)
XLA Ops:
  3.4 1.2 fusion.242
  5.3 7.8 %collective-permute-start.1 = (bf16[2,48,256]{2,1,0:T(8,128)(2,1)}, bf16[2,48,256]{2,1,0:T(8,128)(2,1)}, u32[]{:S(2)}, u32[]{:S(2)}) collective-permute-start(bf16[2,48,256]{2,1,0:T(8,128)(2,1)} %get-tuple-element.37), channel_id=1, source_target_pairs={{8,0},{16,8},{24,16},{32,24},{40,32},{48,40},{56,48},{64,56},{72,6... | collective-permute-start | bytes 147464 | tf_op jit(solution)/shard_map/ppermute | solution.py:20
  13.1 1.9 %collective-permute-start = (bf16[2,48,256]{2,1,0:T(8,128)(2,1)}, bf16[2,48,256]{2,1,0:T(8,128)(2,1)}, u32[]{:S(2)}, u32[]{:S(2)}) collective-permute-start(bf16[2,48,256]{2,1,0:T(8,128)(2,1)} %get-tuple-element.36), channel_id=1, source_target_pairs={{0,8},{8,16},{16,24},{24,32},{32,40},{40,48},{48,56},{56,64},{64,7... | collective-permute-start | bytes 147464 | tf_op jit(solution)/shard_map/ppermute | solution.py:17
  16.4 1.9 %collective-permute-start.2 = (f32[20,48]{1,0:T(8,128)}, f32[20,48]{1,0:T(8,128)S(1)}, u32[]{:S(2)}, u32[]{:S(2)}) collective-permute-start(f32[20,48]{1,0:T(8,128)} %get-tuple-element.55), channel_id=1, source_target_pairs={{0,8},{8,16},{16,24},{24,32},{32,40},{40,48},{48,56},{56,64},{64,7... | collective-permute-start | bytes 11528 | tf_op jit(solution)/shard_map/ppermute | solution.py:17
  18.3 6.7 %collective-permute-start.3 = (f32[20,48]{1,0:T(8,128)}, f32[20,48]{1,0:T(8,128)}, u32[]{:S(2)}, u32[]{:S(2)}) collective-permute-start(f32[20,48]{1,0:T(8,128)} %get-tuple-element.54), channel_id=1, source_target_pairs={{8,0},{16,8},{24,16},{32,24},{40,32},{48,40},{56,48},{64,56},{72,6... | collective-permute-start | bytes 11528 | tf_op jit(solution)/shard_map/ppermute | solution.py:20
  29.6 1.3 slice_bitcast_fusion.23
  55.6 29.9 %all_gather.3 = bf16[3,8,4,32,128]{4,3,2,0,1:T(8,128)(2,1)S(1)} all-gather(bf16[3,1,4,32,128]{4,3,2,0,1:T(8,128)(2,1)S(1)} %copy.198), channel_id=1, replica_groups=mesh['atom'=32,'sample'=8] {'sample'}, dimensions={1}, use_global_device_ids=true | all-gather | bytes 884736 | tf_op jit(solution)/shard_map/all_gather | solution.py:129
  89.4 1.3 fusion.14
  91.7 4.6 %convolution_bitcast_fusion.2 = f32[2,8,32,4,32]{2,4,3,1,0:T(8,128)} fusion(bf16[2,8,128,4,32]{2,4,3,1,0:T(8,128)(2,1)S(1)} %bitcast.277, f32[2,8,4,32]{3,2,1,0:T(4,128)S(1)} %fusion.244, f32[2,8,4,32,128]{4,3,2,1,0:T(8,128)S(1)} %fusion.14), kind=kOutput, calls=%fused_computation.17 | convolution fusion | flops 17565824 | bytes 1843200 | tf_op jit(solution)/shard_map/swhqk,swkhd->swqhd/dot_general | solution.py:165
  96.4 1.6 %copy.199 = f32[2,8,32,4,32]{4,3,2,1,0:T(4,128)S(1)} copy(f32[2,8,32,4,32]{2,4,3,1,0:T(8,128)} %convolution_bitcast_fusion.2) | data formatting | bytes 524288 | tf_op jit(solution)/shard_map/swhqk,swkhd->swqhd/transpose | solution.py:165
  101.1 1.3 fusion.89
  104.5 1.2 fusion.247
  105.8 1.9 %collective-permute-start.5 = (bf16[2,48,256]{2,1,0:T(8,128)(2,1)S(1)}, bf16[2,48,256]{2,1,0:T(8,128)(2,1)S(1)}, u32[]{:S(2)}, u32[]{:S(2)}) collective-permute-start(bf16[2,48,256]{2,1,0:T(8,128)(2,1)S(1)} %get-tuple-element.35), channel_id=1, source_target_pairs={{8,0},{16,8},{24,16},{32,24},{40,32},{48,40},{56,48},{64,56},{72,6... | collective-permute-start | bytes 147464 | tf_op jit(solution)/shard_map/ppermute | solution.py:20
  107.7 2.6 %collective-permute-start.4 = (bf16[2,48,256]{2,1,0:T(8,128)(2,1)S(1)}, bf16[2,48,256]{2,1,0:T(8,128)(2,1)S(1)}, u32[]{:S(2)}, u32[]{:S(2)}) collective-permute-start(bf16[2,48,256]{2,1,0:T(8,128)(2,1)S(1)} %get-tuple-element.34), channel_id=1, source_target_pairs={{0,8},{8,16},{16,24},{24,32},{32,40},{40,48},{48,56},{56,64},{64,7... | collective-permute-start | bytes 147464 | tf_op jit(solution)/shard_map/ppermute | solution.py:17
  111.2 5.0 %collective-permute-done.4 = bf16[2,48,256]{2,1,0:T(8,128)(2,1)S(1)} collective-permute-done((bf16[2,48,256]{2,1,0:T(8,128)(2,1)S(1)}, bf16[2,48,256]{2,1,0:T(8,128)(2,1)S(1)}, u32[]{:S(2)}, u32[]{:S(2)}) %collective-permute-start.4) | collective-permute-done | bytes 49184 | tf_op jit(solution)/shard_map/ppermute | solution.py:17
  119.5 4.6 %convolution_bitcast_fusion.1 = f32[2,8,32,4,32]{2,4,3,1,0:T(8,128)} fusion(bf16[2,8,128,4,32]{2,4,3,1,0:T(8,128)(2,1)S(1)} %bitcast.278, f32[2,8,4,32]{3,2,1,0:T(4,128)S(1)} %fusion.248, f32[2,8,4,32,128]{4,3,2,1,0:T(8,128)S(1)} %fusion.12), kind=kOutput, calls=%fused_computation.13 | convolution fusion | flops 17565824 | bytes 1843200 | tf_op jit(solution)/shard_map/swhqk,swkhd->swqhd/dot_general | solution.py:165
  124.1 1.6 %copy.216 = f32[2,8,32,4,32]{4,3,2,1,0:T(4,128)S(1)} copy(f32[2,8,32,4,32]{2,4,3,1,0:T(8,128)} %convolution_bitcast_fusion.1) | data formatting | bytes 524288 | tf_op jit(solution)/shard_map/swhqk,swkhd->swqhd/transpose | solution.py:165
  128.8 1.3 fusion.91
  133.5 1.9 %collective-permute-start.7 = (bf16[2,48,256]{2,1,0:T(8,128)(2,1)S(1)}, bf16[2,48,256]{2,1,0:T(8,128)(2,1)S(1)}, u32[]{:S(2)}, u32[]{:S(2)}) collective-permute-start(bf16[2,48,256]{2,1,0:T(8,128)(2,1)S(1)} %get-tuple-element.33), channel_id=1, source_target_pairs={{8,0},{16,8},{24,16},{32,24},{40,32},{48,40},{56,48},{64,56},{72,6... | collective-permute-start | bytes 147464 | tf_op jit(solution)/shard_map/ppermute | solution.py:20
  135.5 2.4 %collective-permute-start.6 = (bf16[2,48,256]{2,1,0:T(8,128)(2,1)S(1)}, bf16[2,48,256]{2,1,0:T(8,128)(2,1)S(1)}, u32[]{:S(2)}, u32[]{:S(2)}) collective-permute-start(bf16[2,48,256]{2,1,0:T(8,128)(2,1)S(1)} %get-tuple-element.32), channel_id=1, source_target_pairs={{0,8},{8,16},{16,24},{24,32},{32,40},{40,48},{48,56},{56,64},{64,7... | collective-permute-start | bytes 147464 | tf_op jit(solution)/shard_map/ppermute | solution.py:17
  138.8 5.1 %collective-permute-done.6 = bf16[2,48,256]{2,1,0:T(8,128)(2,1)S(1)} collective-permute-done((bf16[2,48,256]{2,1,0:T(8,128)(2,1)S(1)}, bf16[2,48,256]{2,1,0:T(8,128)(2,1)S(1)}, u32[]{:S(2)}, u32[]{:S(2)}) %collective-permute-start.6) | collective-permute-done | bytes 49184 | tf_op jit(solution)/shard_map/ppermute | solution.py:17
  146.0 4.6 %convolution_bitcast_fusion = f32[2,8,32,4,32]{2,4,3,1,0:T(8,128)} fusion(bf16[2,8,128,4,32]{2,4,3,1,0:T(8,128)(2,1)S(1)} %bitcast.276, f32[2,8,4,32]{3,2,1,0:T(4,128)S(1)} %fusion.252, f32[2,8,4,32,128]{4,3,2,1,0:T(8,128)S(1)} %fusion.10), kind=kOutput, calls=%fused_computation.9 | convolution fusion | flops 17565824 | bytes 1843200 | tf_op jit(solution)/shard_map/swhqk,swkhd->swqhd/dot_general | solution.py:165
  150.6 1.6 %copy.233 = f32[2,8,32,4,32]{4,3,2,1,0:T(4,128)S(1)} copy(f32[2,8,32,4,32]{2,4,3,1,0:T(8,128)} %convolution_bitcast_fusion) | data formatting | bytes 524288 | tf_op jit(solution)/shard_map/swhqk,swkhd->swqhd/transpose | solution.py:165
  155.4 1.3 fusion.93
  (238 shorter events, 62.8 us)
Async XLA Ops:
  0.0 51.9 %copy-start = (f32[16,9]{1,0:T(8,128)S(1)}, f32[16,9]{1,0:T(8,128)}, u32[]{:S(2)}) copy-start(f32[16,9]{1,0:T(8,128)} %param.20) | copy-start | bytes 1732
  0.0 1.0 copy-start.1
  4.6 28.0 %copy-start.2 = (f32[2,256,512]{2,1,0:T(8,128)}, f32[2,256,512]{2,1,0:T(8,128)S(1)}, u32[]{:S(2)}) copy-start(f32[2,256,512]{2,1,0:T(8,128)S(1)} %get-tuple-element.65) | copy-start | bytes 3145732
  4.6 10.4 %copy-start.37 = (bf16[2,128,16]{1,2,0:T(8,128)(2,1)S(1)}, bf16[2,128,16]{1,2,0:T(8,128)(2,1)}, u32[]{:S(2)}) copy-start(bf16[2,128,16]{1,2,0:T(8,128)(2,1)} %param.21) | copy-start | bytes 24580
  5.3 81.3 %collective-permute-start.1 = (bf16[2,48,256]{2,1,0:T(8,128)(2,1)}, bf16[2,48,256]{2,1,0:T(8,128)(2,1)}, u32[]{:S(2)}, u32[]{:S(2)}) collective-permute-start(bf16[2,48,256]{2,1,0:T(8,128)(2,1)} %get-tuple-element.37), channel_id=1, source_target_pairs={{8,0},{16,8},{24,16},{32,24},{40,32},{48,40},{56,48},{64,56},{72,6... | collective-permute-start | bytes 147464 | tf_op jit(solution)/shard_map/ppermute | solution.py:20
  13.1 2.1 %copy-start.43 = (s32[256]{0:T(256)S(1)}, s32[256]{0:T(256)}, u32[]{:S(2)}) copy-start(s32[256]{0:T(256)} %param.18) | copy-start | bytes 3076
  13.1 73.5 %collective-permute-start = (bf16[2,48,256]{2,1,0:T(8,128)(2,1)}, bf16[2,48,256]{2,1,0:T(8,128)(2,1)}, u32[]{:S(2)}, u32[]{:S(2)}) collective-permute-start(bf16[2,48,256]{2,1,0:T(8,128)(2,1)} %get-tuple-element.36), channel_id=1, source_target_pairs={{0,8},{8,16},{16,24},{24,32},{32,40},{40,48},{48,56},{56,64},{64,7... | collective-permute-start | bytes 147464 | tf_op jit(solution)/shard_map/ppermute | solution.py:17
  16.4 32.2 %collective-permute-start.2 = (f32[20,48]{1,0:T(8,128)}, f32[20,48]{1,0:T(8,128)S(1)}, u32[]{:S(2)}, u32[]{:S(2)}) collective-permute-start(f32[20,48]{1,0:T(8,128)} %get-tuple-element.55), channel_id=1, source_target_pairs={{0,8},{8,16},{16,24},{24,32},{32,40},{40,48},{48,56},{56,64},{64,7... | collective-permute-start | bytes 11528 | tf_op jit(solution)/shard_map/ppermute | solution.py:17
  18.3 30.3 %collective-permute-start.3 = (f32[20,48]{1,0:T(8,128)}, f32[20,48]{1,0:T(8,128)}, u32[]{:S(2)}, u32[]{:S(2)}) collective-permute-start(f32[20,48]{1,0:T(8,128)} %get-tuple-element.54), channel_id=1, source_target_pairs={{8,0},{16,8},{24,16},{32,24},{40,32},{48,40},{56,48},{64,56},{72,6... | collective-permute-start | bytes 11528 | tf_op jit(solution)/shard_map/ppermute | solution.py:20
  27.0 1.2 copy-start.42
  29.0 4.4 %copy-start.34 = (f32[20,1,32]{2,1,0:T(1,128)}, f32[20,1,32]{2,1,0:T(1,128)S(1)}, u32[]{:S(2)}) copy-start(f32[20,1,32]{2,1,0:T(1,128)S(1)} %fusion.202) | copy-start | bytes 7684
  33.4 1.7 %copy-start.11 = (f32[256,128]{1,0:T(8,128)S(1)}, f32[256,128]{1,0:T(8,128)}, u32[]{:S(2)}) copy-start(f32[256,128]{1,0:T(8,128)} %get-tuple-element.31) | copy-start | bytes 393220
  90.7 1.0 copy-start.20
  100.1 1.0 copy-start.27
  101.1 1.3 copy-start.32
  105.8 5.2 %copy-start.4 = (f32[2,256,512]{2,1,0:T(8,128)}, f32[2,256,512]{2,1,0:T(8,128)S(1)}, u32[]{:S(2)}) copy-start(f32[2,256,512]{2,1,0:T(8,128)S(1)} %get-tuple-element.73) | copy-start | bytes 3145732
  105.8 5.4 %collective-permute-start.5 = (bf16[2,48,256]{2,1,0:T(8,128)(2,1)S(1)}, bf16[2,48,256]{2,1,0:T(8,128)(2,1)S(1)}, u32[]{:S(2)}, u32[]{:S(2)}) collective-permute-start(bf16[2,48,256]{2,1,0:T(8,128)(2,1)S(1)} %get-tuple-element.35), channel_id=1, source_target_pairs={{8,0},{16,8},{24,16},{32,24},{40,32},{48,40},{56,48},{64,56},{72,6... | collective-permute-start | bytes 147464 | tf_op jit(solution)/shard_map/ppermute | solution.py:20
  107.7 8.5 %collective-permute-start.4 = (bf16[2,48,256]{2,1,0:T(8,128)(2,1)S(1)}, bf16[2,48,256]{2,1,0:T(8,128)(2,1)S(1)}, u32[]{:S(2)}, u32[]{:S(2)}) collective-permute-start(bf16[2,48,256]{2,1,0:T(8,128)(2,1)S(1)} %get-tuple-element.34), channel_id=1, source_target_pairs={{0,8},{8,16},{16,24},{24,32},{32,40},{40,48},{48,56},{56,64},{64,7... | collective-permute-start | bytes 147464 | tf_op jit(solution)/shard_map/ppermute | solution.py:17
  118.5 1.0 copy-start.21
  128.8 1.3 copy-start.30
  133.5 5.0 %copy-start.3 = (f32[2,256,512]{2,1,0:T(8,128)}, f32[2,256,512]{2,1,0:T(8,128)S(1)}, u32[]{:S(2)}) copy-start(f32[2,256,512]{2,1,0:T(8,128)S(1)} %get-tuple-element.79) | copy-start | bytes 3145732
  133.5 5.3 %collective-permute-start.7 = (bf16[2,48,256]{2,1,0:T(8,128)(2,1)S(1)}, bf16[2,48,256]{2,1,0:T(8,128)(2,1)S(1)}, u32[]{:S(2)}, u32[]{:S(2)}) collective-permute-start(bf16[2,48,256]{2,1,0:T(8,128)(2,1)S(1)} %get-tuple-element.33), channel_id=1, source_target_pairs={{8,0},{16,8},{24,16},{32,24},{40,32},{48,40},{56,48},{64,56},{72,6... | collective-permute-start | bytes 147464 | tf_op jit(solution)/shard_map/ppermute | solution.py:20
  135.5 8.4 %collective-permute-start.6 = (bf16[2,48,256]{2,1,0:T(8,128)(2,1)S(1)}, bf16[2,48,256]{2,1,0:T(8,128)(2,1)S(1)}, u32[]{:S(2)}, u32[]{:S(2)}) collective-permute-start(bf16[2,48,256]{2,1,0:T(8,128)(2,1)S(1)} %get-tuple-element.32), channel_id=1, source_target_pairs={{0,8},{8,16},{16,24},{24,32},{32,40},{40,48},{48,56},{56,64},{64,7... | collective-permute-start | bytes 147464 | tf_op jit(solution)/shard_map/ppermute | solution.py:17
  155.4 1.3 copy-start.28
  (35 other events, 28.8 us)
where the time goes:
time: 160 us; the launch traced here: 159 us
  local copies, waits for them, and re-layouts  44.7 us (28%)
  matrix products  36.6 us (23%)
  blocking collectives  29.9 us (19%)
  starting transfers between devices  27.1 us (17%)
  waiting for transfers between devices  10.1 us (6%)
  other arithmetic  9.14 us (6%)
    all_gather x1, blocking collectives, local(): attn_bias = lax.all_gather(my_bias, 'sample', axis=1, tiled=True)  29.9 us
    ppermute x4, starting transfers between devices, with_halo(): lax.ppermute(lax.slice_in_dim(block, 0, width, axis=dim), axis, backward)  18.3 us
    unnamed x100, local copies, waits for them, and re-layouts  14.4 us
    dot_general x3, matrix products, local(): jnp.einsum('swhqk,swkhd->swqhd', attn_probs, value_heads, preferred_eleme...  13.9 us
    ppermute x4, waiting for transfers between devices, with_halo(): lax.ppermute(lax.slice_in_dim(block, block.shape[dim] - width, None, axis...  10 us
    ppermute x4, starting transfers between devices, with_halo(): lax.ppermute(lax.slice_in_dim(block, block.shape[dim] - width, None, axis...  8.82 us
    div x12, local copies, waits for them, and re-layouts, local(): jax.nn.sigmoid(cond_values[:, 0:channels]) * layer_norm(residual)  8.4 us
    transpose x3, local copies, waits for them, and re-layouts, local(): jnp.einsum('swhqk,swkhd->swqhd', attn_probs, value_heads, preferred_eleme...  4.88 us
  transfers between devices with their start and end apart: 8, of which 2 were waited for; matrix products, arithmetic and copies ran while one was open for 17% of the time, Pallas kernels for 0%

commit v1 on v0

--- a/solution.py
+++ b/solution.py
@@ -7,6 +7,11 @@
 KW = 128
 REL_CLIP = 4
 NREL = 9
+
+
+def exchange_gather(x, axis, dim):
+    stack = jnp.stack([x] * lax.axis_size(axis))
+    return jnp.concatenate(lax.all_to_all(stack, axis, 0, 0), axis=dim)
 
 
 def with_halo(block, sides, width):
@@ -126,7 +131,7 @@
     my_keys = key_windows(key_block, share_count, 1)
     my_valid = lax.dynamic_slice_in_dim(key_valid, first_window, share_count, 0)
     my_bias = pair_bias(my_queries, my_keys, my_valid, w_pair_in, w_rel, w_pair_mlp, w_bias)
-    attn_bias = lax.all_gather(my_bias, "sample", axis=1, tiled=True)
+    attn_bias = exchange_gather(my_bias, "sample", 1)
     scale_factor = head_dim ** (-0.5)
     residual = atom_act.astype(jnp.float32)
     for layer_index in range(w_attn.shape[0]):

time: 160 us -> 128 us (0.80)
  blocking collectives: 29.9 us -> 0 us
  starting transfers between devices: 27.1 us -> 33.6 us
  matrix products: 36.6 us -> 31.7 us
  local copies, waits for them, and re-layouts: 44.7 us -> 39.9 us
    all_gather x1 -> x0, blocking collectives: 29.9 us -> none  [local(): attn_bias = lax.all_gather(my_bias, 'sample', axis=1, tiled=True)]
    all_to_all x0 -> x1, starting transfers between devices: none -> 5.36 us  [exchange_gather(): return jnp.concatenate(lax.all_to_all(stack, axis, 0, 0), axis=dim)]
    transpose x3, local copies, waits for them, and re-layouts: 4.88 us -> 1.24 us  [local(): jnp.einsum('swhqk,swkhd->swqhd', attn_probs, value_heads, preferred_eleme...]
    dot_general x3, matrix products: 13.9 us -> 10.9 us  [local(): jnp.einsum('swhqk,swkhd->swqhd', attn_probs, value_heads, preferred_eleme...]
    dot_general x3, matrix products: 3.51 us -> 1.64 us  [local(): jnp.dot(atom_cond, w_cond[layer_index], preferred_element_type=jnp.float32)]
    unnamed x100 -> x96, local copies, waits for them, and re-layouts: 14.4 us -> 13.9 us
  transfers between devices with their start and end apart: 8 -> 9, of which waited for: 2 -> 2; matrix products, arithmetic and copies ran while one was open for 17% -> 20% of each run, Pallas kernels for 0% -> 0%
where the time goes in v1:
time: 128 us; the launch traced here: 126 us
  local copies, waits for them, and re-layouts  39.9 us (31%)
  starting transfers between devices  33.6 us (26%)
  matrix products  31.7 us (25%)
  waiting for transfers between devices  11.1 us (9%)
  other arithmetic  8.79 us (7%)
    ppermute x4, starting transfers between devices, with_halo(): lax.ppermute(lax.slice_in_dim(block, 0, width, axis=dim), axis, backward)  19.9 us
    unnamed x96, local copies, waits for them, and re-layouts  13.9 us
    ppermute x4, waiting for transfers between devices, with_halo(): lax.ppermute(lax.slice_in_dim(block, block.shape[dim] - width, None, axis...  11.1 us
    dot_general x3, matrix products, local(): jnp.einsum('swhqk,swkhd->swqhd', attn_probs, value_heads, preferred_eleme...  10.9 us
    div x12, local copies, waits for them, and re-layouts, local(): jax.nn.sigmoid(cond_values[:, 0:channels]) * layer_norm(residual)  8.36 us
    ppermute x4, starting transfers between devices, with_halo(): lax.ppermute(lax.slice_in_dim(block, block.shape[dim] - width, None, axis...  8.34 us
    all_to_all x1, starting transfers between devices, exchange_gather(): return jnp.concatenate(lax.all_to_all(stack, axis, 0, 0), axis=dim)  5.36 us
    dot_general x3, matrix products, local(): jnp.einsum('sac,cf->saf', modulated, weights, preferred_element_type=jnp....  4.73 us
  transfers between devices with their start and end apart: 9, of which 2 were waited for; matrix products, arithmetic and copies ran while one was open for 20% of the time, Pallas kernels for 0%

profile of v1, /device:TPU:30, one launch (start us, length us, event | category | flops | bytes accessed | tf_op | source)
XLA Modules:
  0.0 126.1 jit_solution(5404360250939047675)
XLA Ops:
  1.1 1.2 fusion.81
  3.4 2.3 %fusion.242 = (bf16[2,256,512]{2,1,0:T(8,128)(2,1)S(1)}, f32[2,256,512]{2,1,0:T(8,128)}) fusion(bf16[3,128,512]{2,1,0:T(8,128)(2,1)} %param.25, bf16[2,256,128]{1,2,0:T(8,128)(2,1)S(1)} %copy.178, f32[256,128]{0,1:T(8,128)S(1)} %copy.181, f32[2,256]{1,0:T(2,128)S(1)} %add_rsqrt_fusion.5, f32[2,256]{1,0:T(2,128)S(1)} %broadcast_multiply_fusion.6, ...), kind=kOutput, calls=%fused_computation.360 | convolution fusion | flops 67764224 | bytes 2101248 | tf_op jit(solution)/shard_map/sac,cf->saf/dot_general | solution.py:144
  6.3 7.8 %collective-permute-start.1 = (bf16[2,48,256]{2,1,0:T(8,128)(2,1)}, bf16[2,48,256]{2,1,0:T(8,128)(2,1)S(1)}, u32[]{:S(2)}, u32[]{:S(2)}) collective-permute-start(bf16[2,48,256]{2,1,0:T(8,128)(2,1)} %get-tuple-element.37), channel_id=1, source_target_pairs={{8,0},{16,8},{24,16},{32,24},{40,32},{48,40},{56,48},{64,56},{72,6... | collective-permute-start | bytes 147464 | tf_op jit(solution)/shard_map/ppermute | solution.py:25
  14.1 1.9 %collective-permute-start = (bf16[2,48,256]{2,1,0:T(8,128)(2,1)}, bf16[2,48,256]{2,1,0:T(8,128)(2,1)}, u32[]{:S(2)}, u32[]{:S(2)}) collective-permute-start(bf16[2,48,256]{2,1,0:T(8,128)(2,1)} %get-tuple-element.36), channel_id=1, source_target_pairs={{0,8},{8,16},{16,24},{24,32},{32,40},{40,48},{48,56},{56,64},{64,7... | collective-permute-start | bytes 147464 | tf_op jit(solution)/shard_map/ppermute | solution.py:22
  16.9 1.9 %collective-permute-start.2 = (f32[20,48]{1,0:T(8,128)S(1)}, f32[20,48]{1,0:T(8,128)S(1)}, u32[]{:S(2)}, u32[]{:S(2)}) collective-permute-start(f32[20,48]{1,0:T(8,128)S(1)} %get-tuple-element.55), channel_id=1, source_target_pairs={{0,8},{8,16},{16,24},{24,32},{32,40},{40,48},{48,56},{56,64},{64,7... | collective-permute-start | bytes 11528 | tf_op jit(solution)/shard_map/ppermute | solution.py:22
  18.8 6.7 %collective-permute-start.3 = (f32[20,48]{1,0:T(8,128)S(1)}, f32[20,48]{1,0:T(8,128)S(1)}, u32[]{:S(2)}, u32[]{:S(2)}) collective-permute-start(f32[20,48]{1,0:T(8,128)S(1)} %get-tuple-element.54), channel_id=1, source_target_pairs={{8,0},{16,8},{24,16},{32,24},{40,32},{48,40},{56,48},{64,56},{72,6... | collective-permute-start | bytes 11528 | tf_op jit(solution)/shard_map/ppermute | solution.py:25
  34.8 5.4 %all-to-all-start = ((bf16[8,3,1,4,32,128]{5,4,3,2,1,0:T(8,128)(2,1)}), bf16[8,3,1,4,32,128]{5,4,3,2,1,0:T(8,128)(2,1)S(1)}, u32[]{:S(2)}, u32[]{:S(2)}) async-start(bf16[8,3,1,4,32,128]{5,4,3,2,1,0:T(8,128)(2,1)} %stack.81), calls=%async_computation | async-start | bytes 1572864 | tf_op jit(solution)/shard_map/all_to_all | solution.py:14
  62.4 3.6 %convolution_bitcast_fusion.2 = f32[2,8,32,4,32]{2,4,3,1,0:T(8,128)S(1)} fusion(bf16[2,8,128,4,32]{2,4,3,1,0:T(8,128)(2,1)S(1)} %bitcast.280, f32[2,8,4,32]{3,2,1,0:T(4,128)S(1)} %fusion.244, f32[2,8,4,32,128]{4,3,2,1,0:T(8,128)S(1)} %fusion.14), kind=kOutput, calls=%fused_computation.17 | convolution fusion | flops 17565824 | bytes 1843200 | tf_op jit(solution)/shard_map/swhqk,swkhd->swqhd/dot_general | solution.py:170
  67.3 1.2 fusion.245
  69.5 1.3 fusion.89
  73.0 1.2 fusion.247
  74.2 3.5 %collective-permute-start.5 = (bf16[2,48,256]{2,1,0:T(8,128)(2,1)S(1)}, bf16[2,48,256]{2,1,0:T(8,128)(2,1)S(1)}, u32[]{:S(2)}, u32[]{:S(2)}) collective-permute-start(bf16[2,48,256]{2,1,0:T(8,128)(2,1)S(1)} %get-tuple-element.35), channel_id=1, source_target_pairs={{8,0},{16,8},{24,16},{32,24},{40,32},{48,40},{56,48},{64,56},{72,6... | collective-permute-start | bytes 147464 | tf_op jit(solution)/shard_map/ppermute | solution.py:25
  77.7 2.1 %collective-permute-start.4 = (bf16[2,48,256]{2,1,0:T(8,128)(2,1)S(1)}, bf16[2,48,256]{2,1,0:T(8,128)(2,1)S(1)}, u32[]{:S(2)}, u32[]{:S(2)}) collective-permute-start(bf16[2,48,256]{2,1,0:T(8,128)(2,1)S(1)} %get-tuple-element.34), channel_id=1, source_target_pairs={{0,8},{8,16},{16,24},{24,32},{32,40},{40,48},{48,56},{56,64},{64,7... | collective-permute-start | bytes 147464 | tf_op jit(solution)/shard_map/ppermute | solution.py:22
  80.8 5.4 %collective-permute-done.4 = bf16[2,48,256]{2,1,0:T(8,128)(2,1)S(1)} collective-permute-done((bf16[2,48,256]{2,1,0:T(8,128)(2,1)S(1)}, bf16[2,48,256]{2,1,0:T(8,128)(2,1)S(1)}, u32[]{:S(2)}, u32[]{:S(2)}) %collective-permute-start.4) | collective-permute-done | bytes 49184 | tf_op jit(solution)/shard_map/ppermute | solution.py:22
  90.2 3.6 %convolution_bitcast_fusion.1 = f32[2,8,32,4,32]{2,4,3,1,0:T(8,128)S(1)} fusion(bf16[2,8,128,4,32]{2,4,3,1,0:T(8,128)(2,1)S(1)} %bitcast.282, f32[2,8,4,32]{3,2,1,0:T(4,128)S(1)} %fusion.248, f32[2,8,4,32,128]{4,3,2,1,0:T(8,128)S(1)} %fusion.12), kind=kOutput, calls=%fused_computation.13 | convolution fusion | flops 17565824 | bytes 1843200 | tf_op jit(solution)/shard_map/swhqk,swkhd->swqhd/dot_general | solution.py:170
  95.2 1.2 fusion.249
  97.4 1.3 %fusion.91 = f32[2,256,512]{2,1,0:T(8,128)S(1)} fusion(f32[2,256,128]{1,2,0:T(8,128)S(1)} %get-tuple-element.75, bf16[3,128,512]{2,1,0:T(8,128)(2,1)} %param.28, f32[256,128]{0,1:T(8,128)S(1)} %copy-done.27, f32[2,256]{1,0:T(2,128)S(1)} %add_rsqrt_fusion.2, f32[2,256]{1,0:T(2,128)S(1)} %broadcast_multiply_fusion.3, f32[256,128]{0,1:T(8,128)S(1)} %copy-done.28), kind=kOutput, calls=%fused_computation.151 | convolution fusion | flops 67436544 | bytes 1708032 | tf_op jit(solution)/shard_map/sac,cf->saf/dot_general | solution.py:182
  100.9 1.2 fusion.251
  102.1 1.9 %collective-permute-start.7 = (bf16[2,48,256]{2,1,0:T(8,128)(2,1)S(1)}, bf16[2,48,256]{2,1,0:T(8,128)(2,1)S(1)}, u32[]{:S(2)}, u32[]{:S(2)}) collective-permute-start(bf16[2,48,256]{2,1,0:T(8,128)(2,1)S(1)} %get-tuple-element.33), channel_id=1, source_target_pairs={{8,0},{16,8},{24,16},{32,24},{40,32},{48,40},{56,48},{64,56},{72,6... | collective-permute-start | bytes 147464 | tf_op jit(solution)/shard_map/ppermute | solution.py:25
  104.0 2.4 %collective-permute-start.6 = (bf16[2,48,256]{2,1,0:T(8,128)(2,1)S(1)}, bf16[2,48,256]{2,1,0:T(8,128)(2,1)S(1)}, u32[]{:S(2)}, u32[]{:S(2)}) collective-permute-start(bf16[2,48,256]{2,1,0:T(8,128)(2,1)S(1)} %get-tuple-element.32), channel_id=1, source_target_pairs={{0,8},{8,16},{16,24},{24,32},{32,40},{40,48},{48,56},{56,64},{64,7... | collective-permute-start | bytes 147464 | tf_op jit(solution)/shard_map/ppermute | solution.py:22
  106.8 5.7 %collective-permute-done.6 = bf16[2,48,256]{2,1,0:T(8,128)(2,1)S(1)} collective-permute-done((bf16[2,48,256]{2,1,0:T(8,128)(2,1)S(1)}, bf16[2,48,256]{2,1,0:T(8,128)(2,1)S(1)}, u32[]{:S(2)}, u32[]{:S(2)}) %collective-permute-start.6) | collective-permute-done | bytes 49184 | tf_op jit(solution)/shard_map/ppermute | solution.py:22
  115.7 3.6 %convolution_bitcast_fusion = f32[2,8,32,4,32]{2,4,3,1,0:T(8,128)S(1)} fusion(bf16[2,8,128,4,32]{2,4,3,1,0:T(8,128)(2,1)S(1)} %bitcast.281, f32[2,8,4,32]{3,2,1,0:T(4,128)S(1)} %fusion.252, f32[2,8,4,32,128]{4,3,2,1,0:T(8,128)S(1)} %fusion.10), kind=kOutput, calls=%fused_computation.9 | convolution fusion | flops 17565824 | bytes 1843200 | tf_op jit(solution)/shard_map/swhqk,swkhd->swqhd/dot_general | solution.py:170
  120.7 1.2 fusion.253
  122.9 1.3 %fusion.93 = f32[2,256,512]{2,1,0:T(8,128)S(1)} fusion(f32[2,256,128]{1,2,0:T(8,128)S(1)} %get-tuple-element.81, bf16[3,128,512]{2,1,0:T(8,128)(2,1)} %param.28, f32[256,128]{0,1:T(8,128)S(1)} %copy-done.25, f32[2,256]{1,0:T(2,128)S(1)} %add_rsqrt_fusion, f32[2,256]{1,0:T(2,128)S(1)} %broadcast_multiply_fusion.1, f32[256,128]{0,1:T(8,128)S(1)} %copy-done.26), kind=kOutput, calls=%fused_computation.153 | convolution fusion | flops 67436544 | bytes 1708032 | tf_op jit(solution)/shard_map/sac,cf->saf/dot_general | solution.py:182
  (236 shorter events, 56.3 us)
Async XLA Ops:
  0.0 30.6 %copy-start = (f32[16,9]{1,0:T(8,128)S(1)}, f32[16,9]{1,0:T(8,128)}, u32[]{:S(2)}) copy-start(f32[16,9]{1,0:T(8,128)} %param.20) | copy-start | bytes 1732
  0.0 1.0 copy-start.2
  3.4 22.4 %copy-start.5 = (bf16[3,128,768]{2,1,0:T(8,128)(2,1)S(1)}, bf16[3,128,768]{2,1,0:T(8,128)(2,1)}, u32[]{:S(2)}) copy-start(bf16[3,128,768]{2,1,0:T(8,128)(2,1)} %param.24) | copy-start | bytes 1769476
  5.6 10.4 %copy-start.40 = (bf16[2,128,16]{1,2,0:T(8,128)(2,1)S(1)}, bf16[2,128,16]{1,2,0:T(8,128)(2,1)}, u32[]{:S(2)}) copy-start(bf16[2,128,16]{1,2,0:T(8,128)(2,1)} %param.21) | copy-start | bytes 24580
  6.3 51.0 %collective-permute-start.1 = (bf16[2,48,256]{2,1,0:T(8,128)(2,1)}, bf16[2,48,256]{2,1,0:T(8,128)(2,1)S(1)}, u32[]{:S(2)}, u32[]{:S(2)}) collective-permute-start(bf16[2,48,256]{2,1,0:T(8,128)(2,1)} %get-tuple-element.37), channel_id=1, source_target_pairs={{8,0},{16,8},{24,16},{32,24},{40,32},{48,40},{56,48},{64,56},{72,6... | collective-permute-start | bytes 147464 | tf_op jit(solution)/shard_map/ppermute | solution.py:25
  14.1 2.1 %copy-start.44 = (s32[256]{0:T(256)S(1)}, s32[256]{0:T(256)}, u32[]{:S(2)}) copy-start(s32[256]{0:T(256)} %param.18) | copy-start | bytes 3076
  14.1 43.2 %collective-permute-start = (bf16[2,48,256]{2,1,0:T(8,128)(2,1)}, bf16[2,48,256]{2,1,0:T(8,128)(2,1)}, u32[]{:S(2)}, u32[]{:S(2)}) collective-permute-start(bf16[2,48,256]{2,1,0:T(8,128)(2,1)} %get-tuple-element.36), channel_id=1, source_target_pairs={{0,8},{8,16},{16,24},{24,32},{32,40},{40,48},{48,56},{56,64},{64,7... | collective-permute-start | bytes 147464 | tf_op jit(solution)/shard_map/ppermute | solution.py:22
  16.9 12.5 %collective-permute-start.2 = (f32[20,48]{1,0:T(8,128)S(1)}, f32[20,48]{1,0:T(8,128)S(1)}, u32[]{:S(2)}, u32[]{:S(2)}) collective-permute-start(f32[20,48]{1,0:T(8,128)S(1)} %get-tuple-element.55), channel_id=1, source_target_pairs={{0,8},{8,16},{16,24},{24,32},{32,40},{40,48},{48,56},{56,64},{64,7... | collective-permute-start | bytes 11528 | tf_op jit(solution)/shard_map/ppermute | solution.py:22
  18.8 10.6 %collective-permute-start.3 = (f32[20,48]{1,0:T(8,128)S(1)}, f32[20,48]{1,0:T(8,128)S(1)}, u32[]{:S(2)}, u32[]{:S(2)}) collective-permute-start(f32[20,48]{1,0:T(8,128)S(1)} %get-tuple-element.54), channel_id=1, source_target_pairs={{8,0},{16,8},{24,16},{32,24},{40,32},{48,40},{56,48},{64,56},{72,6... | collective-permute-start | bytes 11528 | tf_op jit(solution)/shard_map/ppermute | solution.py:25
  26.4 1.5 %copy-start.37 = (f32[20,1,32]{2,1,0:T(1,128)}, f32[20,1,32]{2,1,0:T(1,128)S(1)}, u32[]{:S(2)}) copy-start(f32[20,1,32]{2,1,0:T(1,128)S(1)} %fusion.202) | copy-start | bytes 7684
  34.8 5.4 %copy-start.43 = (f32[3,128]{1,0:T(4,128)S(1)}, f32[3,128]{1,0:T(4,128)}, u32[]{:S(2)}) copy-start(f32[3,128]{1,0:T(4,128)} %param.26) | copy-start | bytes 4612
  34.8 25.2 %all-to-all-start = ((bf16[8,3,1,4,32,128]{5,4,3,2,1,0:T(8,128)(2,1)}), bf16[8,3,1,4,32,128]{5,4,3,2,1,0:T(8,128)(2,1)S(1)}, u32[]{:S(2)}, u32[]{:S(2)}) async-start(bf16[8,3,1,4,32,128]{5,4,3,2,1,0:T(8,128)(2,1)} %stack.81), calls=%async_computation | async-start | bytes 1572864 | tf_op jit(solution)/shard_map/all_to_all | solution.py:14
  61.3 1.0 copy-start.22
  69.5 1.3 %copy-start.35 = (f32[256,128]{0,1:T(8,128)S(1)}, f32[256,128]{0,1:T(8,128)}, u32[]{:S(2)}) copy-start(f32[256,128]{0,1:T(8,128)} %copy.197) | copy-start | bytes 393220
  74.2 12.1 %copy-start.4 = (f32[2,256,512]{2,1,0:T(8,128)}, f32[2,256,512]{2,1,0:T(8,128)S(1)}, u32[]{:S(2)}) copy-start(f32[2,256,512]{2,1,0:T(8,128)S(1)} %get-tuple-element.73) | copy-start | bytes 3145732
  74.2 6.6 %collective-permute-start.5 = (bf16[2,48,256]{2,1,0:T(8,128)(2,1)S(1)}, bf16[2,48,256]{2,1,0:T(8,128)(2,1)S(1)}, u32[]{:S(2)}, u32[]{:S(2)}) collective-permute-start(bf16[2,48,256]{2,1,0:T(8,128)(2,1)S(1)} %get-tuple-element.35), channel_id=1, source_target_pairs={{8,0},{16,8},{24,16},{32,24},{40,32},{48,40},{56,48},{64,56},{72,6... | collective-permute-start | bytes 147464 | tf_op jit(solution)/shard_map/ppermute | solution.py:25
  77.7 8.5 %collective-permute-start.4 = (bf16[2,48,256]{2,1,0:T(8,128)(2,1)S(1)}, bf16[2,48,256]{2,1,0:T(8,128)(2,1)S(1)}, u32[]{:S(2)}, u32[]{:S(2)}) collective-permute-start(bf16[2,48,256]{2,1,0:T(8,128)(2,1)S(1)} %get-tuple-element.34), channel_id=1, source_target_pairs={{0,8},{8,16},{16,24},{24,32},{32,40},{40,48},{48,56},{56,64},{64,7... | collective-permute-start | bytes 147464 | tf_op jit(solution)/shard_map/ppermute | solution.py:22
  89.2 1.0 copy-start.24
  97.4 1.3 %copy-start.33 = (f32[256,128]{0,1:T(8,128)S(1)}, f32[256,128]{0,1:T(8,128)}, u32[]{:S(2)}) copy-start(f32[256,128]{0,1:T(8,128)} %copy.214) | copy-start | bytes 393220
  102.1 10.4 %copy-start.3 = (f32[2,256,512]{2,1,0:T(8,128)}, f32[2,256,512]{2,1,0:T(8,128)S(1)}, u32[]{:S(2)}) copy-start(f32[2,256,512]{2,1,0:T(8,128)S(1)} %get-tuple-element.79) | copy-start | bytes 3145732
  102.1 4.7 %collective-permute-start.7 = (bf16[2,48,256]{2,1,0:T(8,128)(2,1)S(1)}, bf16[2,48,256]{2,1,0:T(8,128)(2,1)S(1)}, u32[]{:S(2)}, u32[]{:S(2)}) collective-permute-start(bf16[2,48,256]{2,1,0:T(8,128)(2,1)S(1)} %get-tuple-element.33), channel_id=1, source_target_pairs={{8,0},{16,8},{24,16},{32,24},{40,32},{48,40},{56,48},{64,56},{72,6... | collective-permute-start | bytes 147464 | tf_op jit(solution)/shard_map/ppermute | solution.py:25
  104.0 8.4 %collective-permute-start.6 = (bf16[2,48,256]{2,1,0:T(8,128)(2,1)S(1)}, bf16[2,48,256]{2,1,0:T(8,128)(2,1)S(1)}, u32[]{:S(2)}, u32[]{:S(2)}) collective-permute-start(bf16[2,48,256]{2,1,0:T(8,128)(2,1)S(1)} %get-tuple-element.32), channel_id=1, source_target_pairs={{0,8},{8,16},{16,24},{24,32},{32,40},{40,48},{48,56},{56,64},{64,7... | collective-permute-start | bytes 147464 | tf_op jit(solution)/shard_map/ppermute | solution.py:22
  114.7 1.0 copy-start.23
  122.9 1.3 %copy-start.31 = (f32[256,128]{0,1:T(8,128)S(1)}, f32[256,128]{0,1:T(8,128)}, u32[]{:S(2)}) copy-start(f32[256,128]{0,1:T(8,128)} %copy.231) | copy-start | bytes 393220
  (34 other events, 29.7 us)
